TPU v7x, 128 devices: a whole 4x4x4 slice. The times are simulated.
128 devices in a mesh: req: 4 (over y), tok: 32 (over z, x, core).
Axes of the slice: x: 4, y: 4, z: 4, core: 2. Of those that a mesh axis runs over, the one named last changes fastest.
Arguments:
- tokens: bfloat16 [8, 2048, 1536], P('req', 'tok'), may hold values from -16 to 16
- gain_attn: float32 [1536], replicated, may hold values from 0.1 to 1.9
- query_weight: bfloat16 [1536, 1536], replicated, may hold values from -0.375 to 0.375
- key_value_weight: bfloat16 [1536, 1024], replicated, may hold values from -0.15625 to 0.15625
- w_out: bfloat16 [1536, 1536], replicated, may hold values from -0.15625 to 0.15625
- kv_pool: bfloat16 [512, 64, 1024], P(('req', 'tok')), may hold values from -170 to 170, as said below
- migrate: int32 [512], P(('req', 'tok')), may hold values from 0 to 511, as said below
- page_table: int32 [8, 64], P('req'), may hold values from 0 to 127, as said below
- cache_len: int32 [8], P('req'), may hold values from 0 to 4096, as said below
- gain_ffn: float32 [1536], replicated, may hold values from 0.1 to 1.9
- routes: int32 [8, 2048, 8], P('req', 'tok'), may hold values from 0 to 31, all different within a row; in each aligned block of 64 rows (0 to 63, 64 to 127, ..., all dimensions but the last counted through in order) at most 24 rows name the same one
- gate_weights: float32 [8, 2048, 8], P('req', 'tok'), may hold values from 0.05 to 0.5
- w_gate_up: bfloat16 [32, 1536, 1024], P('tok'), may hold values from -0.15625 to 0.15625
- w_down: bfloat16 [32, 512, 1536], P('tok'), may hold values from -0.25 to 0.25
Outputs:
- attended: bfloat16 [8, 2048, 1536], P('req', 'tok')
- expert_mix: bfloat16 [8, 2048, 1536], P('req', 'tok')
Inputs may be any that keep to these rules, and one draw needn't show every extreme that they name: `kv_pool`: the values of the cached keys and values. `migrate`: A permutation of all slots that keeps a slot's tok index: slot a*128 + t*4 + i goes to some a2*128 + t*4 + i2. `page_table`: the rows of the 2 requests of one group together hold every slot of the group's pool exactly once. `cache_len`: each length lies within 128 of 0 or of 4096; some request has exactly 4096. `routes`: the 8 experts of a token differ; in each aligned block of 64 rows (one request's tokens on one device) no expert is named more than 24 times.
All inputs are finite; a program needn't handle non-finite values.
Results may differ from a plain program's by a relative error of at most 0.025.
Values may be sent and summed in bfloat16 or wider, within the bound.
No kernel may reach another device: no remote copies, remote signals or barrier semaphores. Data moves between devices by JAX's collectives and lax.ppermute only.
A program may use at most 192 MiB of HBM per device.

v0:
```python
import jax
import jax.numpy as jnp
from jax import lax
from jax.sharding import PartitionSpec as P

QUERY_HEADS = 24
KEY_VALUE_HEADS = 8
HEAD_SIZE = 64
FF = 512
TOPK = 8
MOST = 24
score_masked = -1e30
epsilon = 1e-06
far_position = 1 << 30


def rms_norm(values, gain_vec):
    widened = values.astype(jnp.float32)
    inverse = lax.rsqrt(jnp.mean(widened * widened, axis=-1, keepdims=True) + epsilon)
    return (widened * inverse * gain_vec).astype(jnp.bfloat16)


def pick_block(row_total):
    block_len = min(row_total, 1024)
    while row_total % block_len:
        block_len -= 1
    return block_len


def attend(running, head_rows, meta_abs, query_heads, query_abs):
    row_total = head_rows.shape[1]
    block_len = pick_block(row_total)
    blocks = row_total // block_len
    heads_kv = query_heads.shape[0]
    head_dim = query_heads.shape[2]

    def loop_step(index, carried):
        run_max, run_sum, run_acc = carried
        block = lax.dynamic_slice_in_dim(head_rows, index * block_len, block_len, 1)
        abs_block = lax.dynamic_slice_in_dim(meta_abs, index * block_len, block_len, 0)
        visible = (abs_block[None, :] <= query_abs[:, None])[None, :, :]
        scores = jnp.einsum(
            "hqd,hkd->hqk", query_heads, block[:heads_kv], preferred_element_type=jnp.float32
        ) * head_dim ** (-0.5)
        scores = jnp.where(visible, scores, score_masked)
        new_max = jnp.maximum(run_max, jnp.max(scores, axis=-1))
        weight = jnp.where(visible, jnp.exp(scores - new_max[..., None]), 0.0)
        factor = jnp.exp(run_max - new_max)
        run_sum = run_sum * factor + jnp.sum(weight, axis=-1)
        update = jnp.einsum(
            "hqk,hkd->hqd",
            weight.astype(jnp.bfloat16),
            block[heads_kv:],
            preferred_element_type=jnp.float32,
        )
        run_acc = run_acc * factor[..., None] + update
        return (new_max, run_sum, run_acc)

    return lax.fori_loop(0, blocks, loop_step, running)


def pick_member(state, member_id):
    return jax.tree.map(lambda array: array[member_id], state)


def stack_members(states):
    return jax.tree.map(lambda *arrays: jnp.stack(arrays), *states)


def local(
    tokens,
    gain_attn,
    query_weight,
    key_value_weight,
    w_out,
    kv_pool,
    migrate,
    page_table,
    cache_len,
    gain_ffn,
    routes,
    gate_weights,
    w_gate_up,
    w_down,
):
    request_per_shard, tokens_per_shard, model_width = tokens.shape
    local_rows = request_per_shard * tokens_per_shard
    tok_count = lax.axis_size("tok")
    req_count = lax.axis_size("req")
    tok_index = lax.axis_index("tok")
    kv_width = key_value_weight.shape[1]
    groups_per_head = QUERY_HEADS // KEY_VALUE_HEADS
    flat_rows = tokens.reshape(local_rows, model_width)
    normalized_input = rms_norm(flat_rows, gain_attn)
    query_rows = (
        jnp.dot(normalized_input, query_weight, preferred_element_type=jnp.float32)
        .astype(jnp.bfloat16)
        .reshape(request_per_shard, tokens_per_shard, KEY_VALUE_HEADS, groups_per_head, HEAD_SIZE)
    )
    query_heads = query_rows.transpose(0, 2, 3, 1, 4).reshape(
        request_per_shard, KEY_VALUE_HEADS, groups_per_head * tokens_per_shard, HEAD_SIZE
    )
    keyval_pos = (
        jnp.einsum(
            "rcd,dk->crk",
            normalized_input.reshape(request_per_shard, tokens_per_shard, model_width),
            key_value_weight,
            preferred_element_type=jnp.float32,
        )
        .astype(jnp.bfloat16)
        .reshape(tokens_per_shard, request_per_shard * kv_width)
    )
    span_pos = jnp.arange(tokens_per_shard, dtype=jnp.int32)
    query_abs = cache_len[:, None] + tok_index * tokens_per_shard + span_pos[None, :]
    query_abs_rep = jnp.tile(query_abs, (1, groups_per_head))
    pages_dev = kv_pool.shape[0]
    page_rows = kv_pool.shape[1]
    pages_req = page_table.shape[1]
    slots_all = request_per_shard * pages_req
    cache_pos = jnp.arange(pages_req * page_rows, dtype=jnp.int32)
    target = migrate // slots_all * pages_dev + migrate % pages_dev
    places = jnp.arange(req_count * pages_dev, dtype=jnp.int32)
    route_pages = (places[:, None] == target[None, :]).astype(jnp.bfloat16)
    outgoing = jnp.einsum(
        "sp,prk->srk", route_pages, kv_pool, preferred_element_type=jnp.float32
    ).astype(jnp.bfloat16)
    outgoing = outgoing.reshape(req_count, pages_dev, page_rows, kv_width)
    arrived = lax.all_to_all(outgoing, "req", split_axis=0, concat_axis=0, tiled=True)
    migrated = jnp.sum(arrived, axis=0, dtype=jnp.float32).astype(jnp.bfloat16)
    query_count = groups_per_head * tokens_per_shard
    start_state = (
        jnp.full((request_per_shard, KEY_VALUE_HEADS, query_count), score_masked, jnp.float32),
        jnp.zeros((request_per_shard, KEY_VALUE_HEADS, query_count), jnp.float32),
        jnp.zeros((request_per_shard, KEY_VALUE_HEADS, query_count, HEAD_SIZE), jnp.float32),
    )
    pool_all = lax.all_gather(migrated, "tok", axis=0, tiled=True)
    pool_heads = pool_all.reshape(
        pool_all.shape[0], page_rows, 2 * KEY_VALUE_HEADS, HEAD_SIZE
    ).transpose(2, 0, 1, 3)
    results = []
    for member_id in range(request_per_shard):
        rows = jnp.take(pool_heads, page_table[member_id], axis=1).reshape(
            2 * KEY_VALUE_HEADS, pages_req * page_rows, HEAD_SIZE
        )
        cache_abs = jnp.where(cache_pos < cache_len[member_id], cache_pos, far_position)
        results.append(
            attend(
                pick_member(start_state, member_id),
                rows,
                cache_abs,
                query_heads[member_id],
                query_abs_rep[member_id],
            )
        )
    running = stack_members(results)
    piece = lax.all_gather(keyval_pos, "tok", axis=0, tiled=True)
    row_total = piece.shape[0]
    by_member = piece.reshape(
        row_total, request_per_shard, 2 * KEY_VALUE_HEADS, HEAD_SIZE
    ).transpose(1, 2, 0, 3)
    positions = jnp.arange(row_total, dtype=jnp.int32)
    fold_results = []
    for member_id in range(request_per_shard):
        piece_abs = cache_len[member_id] + positions
        fold_results.append(
            attend(
                pick_member(running, member_id),
                by_member[member_id],
                piece_abs,
                query_heads[member_id],
                query_abs_rep[member_id],
            )
        )
    final_state = stack_members(fold_results)
    run_max, run_sum, run_acc = final_state
    normalized_heads = (
        (run_acc / run_sum[..., None])
        .astype(jnp.bfloat16)
        .reshape(request_per_shard, KEY_VALUE_HEADS, groups_per_head, tokens_per_shard, HEAD_SIZE)
    )
    heads_out = normalized_heads.transpose(0, 3, 1, 2, 4).reshape(
        local_rows, QUERY_HEADS * HEAD_SIZE
    )
    projected = jnp.dot(heads_out, w_out, preferred_element_type=jnp.float32)
    attended = projected.astype(jnp.bfloat16)
    residual = (flat_rows.astype(jnp.float32) + projected).astype(jnp.bfloat16)
    normed_ffn = rms_norm(residual, gain_ffn)
    member = jnp.arange(request_per_shard, dtype=jnp.int32)
    experts_total = tok_count * w_gate_up.shape[0]
    route_local = routes.reshape(request_per_shard, tokens_per_shard * TOPK)
    onehot = route_local[..., None] == jnp.arange(experts_total, dtype=jnp.int32)[None, None, :]
    rank_all = jnp.cumsum(onehot.astype(jnp.int32), axis=1) - 1
    rank_of = jnp.sum(jnp.where(onehot, rank_all, 0), axis=2)
    slot_of = route_local * (request_per_shard * MOST) + member[:, None] * MOST + rank_of
    slot_flat = slot_of.reshape(-1)
    capacity = experts_total * request_per_shard * MOST
    token_ids = jnp.arange(local_rows * TOPK, dtype=jnp.int32) // TOPK
    source = jnp.zeros((capacity,), jnp.int32).at[slot_flat].set(token_ids + 1)
    gathered = jnp.take(normed_ffn, jnp.maximum(source - 1, 0), axis=0)
    outbound = jnp.where((source > 0)[:, None], gathered, jnp.zeros_like(gathered)).reshape(
        experts_total, request_per_shard * MOST, model_width
    )
    inbound = lax.all_to_all(outbound, "tok", split_axis=0, concat_axis=1, tiled=True)
    gate_up = jnp.einsum("erd,edf->erf", inbound, w_gate_up, preferred_element_type=jnp.float32)
    hidden = (jax.nn.silu(gate_up[..., :FF]) * gate_up[..., FF:]).astype(jnp.bfloat16)
    expert_out = jnp.einsum(
        "erf,efd->erd", hidden, w_down, preferred_element_type=jnp.float32
    ).astype(jnp.bfloat16)
    returned = lax.all_to_all(expert_out, "tok", split_axis=1, concat_axis=0, tiled=True)
    picked = jnp.take(returned.reshape(capacity, model_width), slot_flat, axis=0).reshape(
        local_rows, TOPK, model_width
    )
    mixture = jnp.einsum(
        "qk,qkd->qd", gate_weights.reshape(local_rows, TOPK), picked.astype(jnp.float32)
    )
    return (
        attended.reshape(request_per_shard, tokens_per_shard, model_width),
        mixture.astype(jnp.bfloat16).reshape(request_per_shard, tokens_per_shard, model_width),
    )


def solution(mesh):
    placed = (
        P("req", "tok", None),
        P(),
        P(),
        P(),
        P(),
        P(("req", "tok"), None, None),
        P(("req", "tok")),
        P("req", None),
        P("req"),
        P(),
        P("req", "tok", None),
        P("req", "tok", None),
        P("tok", None, None),
        P("tok", None, None),
    )
    return jax.shard_map(
        local,
        mesh=mesh,
        in_specs=placed,
        out_specs=(P("req", "tok", None), P("req", "tok", None)),
        check_vma=False,
    )
```

profile of v0, /device:TPU:0, one launch (start us, length us, event | category | flops | bytes accessed | tf_op | source)
XLA Modules:
  0.0 831.7 jit_solution(13190696790973247134)
XLA Ops:
  21.8 30.8 %all_to_all.23 = bf16[4,4,64,1024]{3,1,2,0:T(4,128)(2,1)} all-to-all(bf16[4,4,64,1024]{3,1,2,0:T(4,128)(2,1)S(1)} %copy.95), channel_id=1, replica_groups=mesh['req'=4,'tok'=32] {'req'}, dimensions={0} | all-to-all | bytes 4194304 | tf_op jit(solution)/shard_map/all_to_all | solution.py:128
  101.6 12.4 %copy.105 = bf16[2048,2048]{0,1:T(8,128)(2,1)} copy(bf16[2048,2048]{1,0:T(8,128)(2,1)} %all-gather.5.cloned.1.call-done) | data formatting | bytes 16777216 | tf_op jit(solution)/shard_map/all_gather | solution.py:156
  114.0 6.4 slice_bitcast_fusion.1
  120.4 21.6 %all-gather.3.cloned.1.call-done = bf16[128,64,1024]{2,1,0:T(8,128)(2,1)} async-done(((bf16[4,64,1024]{2,1,0:T(8,128)(2,1)}), bf16[128,64,1024]{2,1,0:T(8,128)(2,1)}) %all-gather.3.cloned.1.call-update) | async-done | bytes 16777232 | tf_op jit(solution)/shard_map/all_gather | solution.py:136
  142.0 23.0 %copy.98 = bf16[128,64,1024]{0,2,1:T(8,128)(2,1)} copy(bf16[128,64,1024]{2,1,0:T(8,128)(2,1)} %all-gather.3.cloned.1.call-done) | data formatting | bytes 33554432 | tf_op jit(solution)/shard_map/all_gather | solution.py:136
  165.1 46.1 %copy.99 = bf16[128,64,16,64]{3,1,0,2:T(8,128)(2,1)} copy(bf16[128,64,16,64]{0,3,2,1:T(8,128)(2,1)} %bitcast.228) | data formatting | bytes 33554432 | tf_op jit(solution)/shard_map/reshape | solution.py:137
  211.1 11.9 %gather_fusion.2 = bf16[64,16,64,64]{3,2,1,0:T(8,128)(2,1)} fusion(bf16[16,128,64,64]{3,2,1,0:T(8,128)(2,1)} %bitcast.226, s32[1024]{0:T(1024)S(1)} %pad_clamp_fusion.2), kind=kCustom, calls=%fused_computation.clone | custom fusion | bytes 16777472 | tf_op jit(solution)/shard_map/jit(_take)/gather | solution.py:142
  223.0 11.9 %gather_fusion.3 = bf16[64,16,64,64]{3,2,1,0:T(8,128)(2,1)} fusion(bf16[16,128,64,64]{3,2,1,0:T(8,128)(2,1)} %bitcast.227, s32[1024]{0:T(1024)S(1)} %pad_clamp_fusion.1), kind=kCustom, calls=%fused_computation.1.clone | custom fusion | bytes 16777472 | tf_op jit(solution)/shard_map/jit(_take)/gather | solution.py:142
  234.9 23.0 %select_bitcast_fusion = (bf16[16,64,64,64]{3,2,0,1:T(8,128)(2,1)}, bf16[16,64,64,64]{3,2,0,1:T(8,128)(2,1)}) fusion(bf16[64,16,64,64]{3,2,1,0:T(8,128)(2,1)} %gather_fusion.3, pred[64]{0:T(512)(128)(4,1)S(1)} %get-tuple-element.895, bf16[64,16,64,64]{3,2,1,0:T(8,128)(2,1)} %gather_fusion.2, pred[64]{0:T(512)(128)(4,1)S(1)} %get-tuple-element.873), kind=kLoop, calls=%fused_computation.91 | loop fusion | flops 8388608 | bytes 33554560 | tf_op jit(solution)/shard_map/jit(_take)/select_n | solution.py:142
  257.9 22.9 %copy.100 = bf16[16,64,64,64]{2,1,3,0:T(8,128)(2,1)} copy(bf16[16,64,64,64]{3,2,0,1:T(8,128)(2,1)} %get-tuple-element.902) | data formatting | bytes 16777216 | tf_op jit(solution)/shard_map/jit(_take)/select_n | solution.py:142
  280.7 22.6 %reshape.410 = bf16[16,4096,64]{1,2,0:T(8,128)(2,1)} reshape(bf16[16,64,64,64]{2,1,3,0:T(8,128)(2,1)} %copy.100) | data formatting | bytes 16777216 | tf_op jit(solution)/shard_map/reshape | solution.py:142
  303.3 60.5 %while.74 = (s32[]{:T(128)}, f32[8,192]{1,0:T(8,128)S(1)}, f32[8,192]{1,0:T(8,128)S(1)}, f32[8,192,64]{1,2,0:T(8,128)}, s32[4096]{0:T(1024)S(1)}, /*index=5*/bf1...) while((s32[]{:T(128)}, f32[8,192]{1,0:T(8,128)S(1)}, ...), condition=%wide.region_5.7_spmd.clone, body=%wide.region_2.6_spmd.clone.sunk | while | flops 423599616 | bytes 24100308 | solution.py:59
  327.8 5.7 fusion.181
  343.0 5.7 fusion.181
  358.1 5.7 fusion.181
  363.9 27.0 %while.72 = (s32[]{:T(128)}, f32[8,192]{1,0:T(8,128)S(1)}, f32[8,192]{1,0:T(8,128)S(1)}, f32[8,192,64]{1,2,0:T(8,128)}, s32[2048]{0:T(1024)S(1)}, /*index=5*/bf1...) while((s32[]{:T(128)}, f32[8,192]{1,0:T(8,128)S(1)}, ...), condition=%wide.region_9.11_spmd.clone, body=%wide.region_6.10_spmd.clone.sunk | while | flops 423496704 | bytes 49266148 | solution.py:59
  391.5 22.9 %copy.108 = bf16[16,64,64,64]{2,1,3,0:T(8,128)(2,1)} copy(bf16[16,64,64,64]{3,2,0,1:T(8,128)(2,1)} %get-tuple-element.901) | data formatting | bytes 16777216 | tf_op jit(solution)/shard_map/jit(_take)/select_n | solution.py:142
  414.4 22.6 %reshape.414 = bf16[16,4096,64]{1,2,0:T(8,128)(2,1)} reshape(bf16[16,64,64,64]{2,1,3,0:T(8,128)(2,1)} %copy.108) | data formatting | bytes 16777216 | tf_op jit(solution)/shard_map/reshape | solution.py:142
  437.0 63.0 %while.75 = (s32[]{:T(128)}, f32[8,192]{1,0:T(8,128)S(1)}, f32[8,192]{1,0:T(8,128)S(1)}, f32[8,192,64]{1,2,0:T(8,128)}, s32[4096]{0:T(1024)}, /*index=5*/bf16[16...) while((s32[]{:T(128)}, f32[8,192]{1,0:T(8,128)S(1)}, ...), condition=%wide.region_13.15_spmd.clone, body=%wide.region_10.14_spmd.clone.sunk | while | flops 423599616 | bytes 24100308 | solution.py:59
  462.7 5.7 fusion.188
  478.5 5.7 fusion.188
  494.3 5.7 fusion.188
  500.0 27.1 %while.73 = (s32[]{:T(128)}, f32[8,192]{1,0:T(8,128)S(1)}, f32[8,192]{1,0:T(8,128)S(1)}, f32[8,192,64]{1,2,0:T(8,128)}, s32[2048]{0:T(1024)S(1)}, /*index=5*/bf1...) while((s32[]{:T(128)}, f32[8,192]{1,0:T(8,128)S(1)}, ...), condition=%wide.region_17.19_spmd.clone, body=%wide.region_14.18_spmd.clone.sunk | while | flops 423496704 | bytes 49266148 | solution.py:59
  545.9 6.2 gather_fusion
  554.9 62.1 %all_to_all.24 = bf16[32,48,1536]{2,1,0:T(8,128)(2,1)S(1)} all-to-all(bf16[32,48,1536]{2,1,0:T(8,128)(2,1)S(1)} %select_select_fusion), channel_id=1, replica_groups=mesh['req'=4,'tok'=32] {'tok'}, dimensions={0} | all-to-all | bytes 9437184 | tf_op jit(solution)/shard_map/all_to_all | solution.py:203
  625.3 52.2 %copy.141 = bf16[1,1536,1536]{2,0,1:T(2,128)(2,1)} copy(bf16[1,1536,1536]{2,1,0:T(8,128)(2,1)S(1)} %fusion.78) | data formatting | bytes 9437184 | tf_op jit(solution)/shard_map/convert_element_type | solution.py:208
  678.1 32.0 %reduce.4 = bf16[1536,1536]{1,0:T(8,128)(2,1)} reduce(bf16[1536,1,1536]{2,1,0:T(2,128)(2,1)} %bitcast.229, bf16[]{:T(256)} %broadcast.485), dimensions={1}, to_apply=%bitcast.192.reduce_sub_computation | reduce | bytes 9437186
  710.0 8.2 reshape.485
  724.2 59.0 %all-to-all-done.2 = bf16[32,2,36864]{2,1,0:T(2,128)(2,1)} async-done(((bf16[32,2,36864]{2,1,0:T(2,128)(2,1)}), bf16[32,2,36864]{2,1,0:T(2,128)(2,1)}, u32[]{:S(2)}, u32[]{:S(2)}) %all-to-all-start.2) | async-done | bytes 4718624 | tf_op jit(solution)/shard_map/all_to_all | solution.py:209
  783.2 20.2 %reshape.486 = bf16[1536,1,1536]{2,1,0:T(2,128)(2,1)} reshape(bf16[32,2,36864]{2,1,0:T(2,128)(2,1)} %all-to-all-done.2) | data formatting | bytes 9437184
  803.4 7.2 copy.139
  810.7 10.2 %gather_fusion.1 = bf16[1024,1536]{1,0:T(8,128)(2,1)} fusion(bf16[1536,1536]{1,0:T(8,128)(2,1)} %bitcast.225, s32[1024]{0:T(1024)S(1)} %broadcast_clamp_fusion), kind=kCustom, calls=%fused_computation.3 | custom fusion | bytes 6295552 | tf_op jit(solution)/shard_map/jit(_take)/gather | solution.py:210
  (262 shorter events, 246.4 us)
Async XLA Ops:
  7.2 609.8 %copy-start = (bf16[1,1536,1024]{2,1,0:T(8,128)(2,1)S(1)}, bf16[1,1536,1024]{2,1,0:T(8,128)(2,1)}, u32[]{:S(2)}) copy-start(bf16[1,1536,1024]{2,1,0:T(8,128)(2,1)} %param.36) | copy-start | bytes 9437188
  7.2 4.8 copy-start.24
  7.2 94.4 %all-gather.5.cloned.1.call-start = ((), (), s32[]{:S(2)}) async-start(), calls=%async_computation.4 | async-start | bytes 8650752 | tf_op jit(solution)/shard_map/all_gather | solution.py:156
  12.0 130.0 %all-gather.3.cloned.1.call-start = ((), (), s32[]{:S(2)}) async-start(), calls=%async_computation.3 | async-start | bytes 17301504 | tf_op jit(solution)/shard_map/all_gather | solution.py:136
  19.4 44.1 %copy-start.3 = (bf16[2,64,1536]{2,1,0:T(8,128)(2,1)S(1)}, bf16[2,64,1536]{2,1,0:T(8,128)(2,1)}, u32[]{:S(2)}) copy-start(bf16[2,64,1536]{2,1,0:T(8,128)(2,1)} %param.24) | copy-start | bytes 1179652
  86.4 27.6 %copy-start.12 = (s32[2,512]{1,0:T(2,128)}, s32[2,512]{1,0:T(2,128)S(1)}, u32[]{:S(2)}) copy-start(s32[2,512]{1,0:T(2,128)S(1)} %fusion.111) | copy-start | bytes 12292
  87.2 26.9 %copy-start.9 = (s32[2,64,8]{1,2,0:T(8,128)}, s32[2,64,8]{1,2,0:T(8,128)S(1)}, u32[]{:S(2)}) copy-start(s32[2,64,8]{1,2,0:T(8,128)S(1)} %broadcast_multiply_fusion) | copy-start | bytes 12292
  87.4 0.6 copy-start.21
  88.0 26.0 %copy-start.17 = (s32[1024,1]{0,1:T(1,128)}, s32[1024,1]{0,1:T(1,128)S(1)}, u32[]{:S(2)}) copy-start(s32[1024,1]{0,1:T(1,128)S(1)} %compare_select_fusion) | copy-start | bytes 12292
  367.0 2.7 copy-start.1
  380.4 2.7 copy-start.1
  414.4 22.6 %copy-start.6 = (f32[8,192]{1,0:T(8,128)S(1)}, f32[8,192]{1,0:T(8,128)}, u32[]{:S(2)}) copy-start(f32[8,192]{1,0:T(8,128)} %custom-call.3) | copy-start | bytes 18436
  414.4 22.6 %copy-start.7 = (f32[8,192]{1,0:T(8,128)S(1)}, f32[8,192]{1,0:T(8,128)}, u32[]{:S(2)}) copy-start(f32[8,192]{1,0:T(8,128)} %custom-call.4) | copy-start | bytes 18436
  414.4 22.6 %copy-start.11 = (s32[64]{0:T(128)S(1)}, s32[64]{0:T(128)}, u32[]{:S(2)}) copy-start(s32[64]{0:T(128)} %get-tuple-element.1177) | copy-start | bytes 772
  437.0 63.0 %copy-start.8 = (s32[2048]{0:T(1024)S(1)}, s32[2048]{0:T(1024)}, u32[]{:S(2)}) copy-start(s32[2048]{0:T(1024)} %iota_add_fusion) | copy-start | bytes 24580
  503.3 2.7 copy-start.2
  516.7 2.7 copy-start.2
  527.1 14.4 %copy-start.4 = (bf16[2,64,1536]{2,1,0:T(8,128)(2,1)S(1)}, bf16[2,64,1536]{2,1,0:T(8,128)(2,1)}, u32[]{:S(2)}) copy-start(bf16[2,64,1536]{2,1,0:T(8,128)(2,1)} %param.24) | copy-start | bytes 1179652
  530.0 15.0 %copy-start.19 = (f32[1536]{0:T(1024)S(1)}, f32[1536]{0:T(1024)}, u32[]{:S(2)}) copy-start(f32[1536]{0:T(1024)} %param.33) | copy-start | bytes 18436
  533.0 12.9 %copy-start.14 = (s32[2048]{0:T(1024)S(1)}, s32[2048]{0:T(1024)}, u32[]{:S(2)}) copy-start(s32[2048]{0:T(1024)} %pad_clamp_fusion) | copy-start | bytes 24580
  541.6 3.4 copy-start.5
  545.9 6.2 copy-start.15
  545.9 6.2 copy-start.16
  617.0 5.4 copy-start.23
  718.3 5.2 copy-start.13
  718.3 5.4 copy-start.10
  718.3 5.5 copy-start.22
  718.3 5.8 copy-start.20
  718.3 5.9 copy-start.18
  718.3 64.9 %all-to-all-start.2 = ((bf16[32,2,36864]{2,1,0:T(2,128)(2,1)}), bf16[32,2,36864]{2,1,0:T(2,128)(2,1)}, u32[]{:S(2)}, u32[]{:S(2)}) async-start(bf16[32,2,36864]{2,1,0:T(2,128)(2,1)} %reshape.485), calls=%async_computation.2 | async-start | bytes 9437184 | tf_op jit(solution)/shard_map/all_to_all | solution.py:209
Sparse Core Ops, SparseCore 0:
  12.1 55.4 all-gather.4
  69.9 72.0 all-gather.2
where the time goes:
time: 845 us; the launch traced here: 832 us
  local copies, waits for them, and re-layouts  372 us (44%)
  matrix products  145 us (17%)
  other arithmetic  120 us (14%)
  blocking collectives  92.9 us (11%)
  waiting for transfers between devices  80.6 us (10%)
  between operations  14.7 us (2%)
    dot_general x12, matrix products, loop_step(): jnp.einsum('hqk,hkd->hqd', weight.astype(jnp.bfloat16), block[heads_kv:],...  68.1 us
    all_to_all x1, blocking collectives, local(): lax.all_to_all(outbound, 'tok', split_axis=0, concat_axis=1, tiled=True)  62.1 us
    all_to_all x1, waiting for transfers between devices, local(): lax.all_to_all(expert_out, 'tok', split_axis=1, concat_axis=0, tiled=True)  59 us
    convert_element_type x1, local copies, waits for them, and re-layouts, local(): expert_out = jnp.einsum('erf,efd->erd', hidden, w_down, preferred_element...  52.2 us
    dot_general x12, matrix products, loop_step(): jnp.einsum('hqd,hkd->hqk', query_heads, block[:heads_kv], preferred_eleme...  52.2 us
    reshape x1, local copies, waits for them, and re-layouts, local(): pool_all.reshape(pool_all.shape[0], page_rows, 2 * KEY_VALUE_HEADS, HEAD_...  46.1 us
    select_n x2, local copies, waits for them, and re-layouts, local(): jnp.take(pool_heads, page_table[member_id], axis=1)  45.8 us
    reshape x2, local copies, waits for them, and re-layouts, local(): jnp.take(pool_heads, page_table[member_id], axis=1)  45.2 us
  transfers between devices with their start and end apart: 3, of which 2 were waited for; matrix products, arithmetic and copies ran while one was open for 9% of the time, Pallas kernels for 0%

commit v1 on v0

--- a/solution.py
+++ b/solution.py
@@ -133,7 +133,9 @@
         jnp.zeros((request_per_shard, KEY_VALUE_HEADS, query_count), jnp.float32),
         jnp.zeros((request_per_shard, KEY_VALUE_HEADS, query_count, HEAD_SIZE), jnp.float32),
     )
-    pool_all = lax.all_gather(migrated, "tok", axis=0, tiled=True)
+    pool_all = jnp.concatenate(
+        lax.all_to_all(jnp.stack([migrated] * lax.axis_size("tok")), "tok", 0, 0), axis=0
+    )
     pool_heads = pool_all.reshape(
         pool_all.shape[0], page_rows, 2 * KEY_VALUE_HEADS, HEAD_SIZE
     ).transpose(2, 0, 1, 3)

time: 845 us -> 988 us (1.17)
  waiting for transfers between devices: 80.6 us -> 241 us
  blocking collectives: 92.9 us -> 59.9 us
  starting transfers between devices: 5.29 us -> 18.1 us
    all_to_all x0 -> x2, waiting for transfers between devices: none -> 167 us  [the longest x1 144 us: local(): lax.all_to_all(jnp.stack([migrated] * lax.axis_size('tok')), 'tok', 0, 0)]
    another operation x2 -> x5, local copies, waits for them, and re-layouts: 0.32 us -> 72.7 us  [the longest x2 66.2 us: local(): pool_all.reshape(pool_all.shape[0], page_rows, 2 * KEY_VALUE_HEADS, HEAD_...]
    reshape x1 -> x0, local copies, waits for them, and re-layouts: 46.1 us -> none  [local(): pool_all.reshape(pool_all.shape[0], page_rows, 2 * KEY_VALUE_HEADS, HEAD_...]
    all_to_all x1 -> x0, blocking collectives: 30.8 us -> none  [local(): lax.all_to_all(outgoing, 'req', split_axis=0, concat_axis=0, tiled=True)]
    all_gather x1 -> x0, local copies, waits for them, and re-layouts: 23 us -> none  [local(): pool_all = lax.all_gather(migrated, 'tok', axis=0, tiled=True)]
    all_gather x1 -> x0, waiting for transfers between devices: 21.6 us -> none  [local(): pool_all = lax.all_gather(migrated, 'tok', axis=0, tiled=True)]
    all_gather x1, waiting for transfers between devices: 0.01 us -> 14.1 us  [local(): piece = lax.all_gather(keyval_pos, 'tok', axis=0, tiled=True)]
    all_to_all x0 -> x2, starting transfers between devices: none -> 12.9 us  [the longest x1 8.34 us: local(): lax.all_to_all(jnp.stack([migrated] * lax.axis_size('tok')), 'tok', 0, 0)]
  transfers between devices with their start and end apart: 3 -> 4, of which waited for: 2 -> 4; matrix products, arithmetic and copies ran while one was open for 9% -> 8% of each run, Pallas kernels for 0% -> 0%
where the time goes in v1:
time: 988 us; the launch traced here: 975 us
  local copies, waits for them, and re-layouts  375 us (38%)
  waiting for transfers between devices  241 us (24%)
  matrix products  145 us (15%)
  other arithmetic  121 us (12%)
  blocking collectives  59.9 us (6%)
  starting transfers between devices  18.1 us (2%)
  between operations  14.6 us (1%)
    all_to_all x1, waiting for transfers between devices, local(): lax.all_to_all(jnp.stack([migrated] * lax.axis_size('tok')), 'tok', 0, 0)  144 us
    dot_general x12, matrix products, loop_step(): jnp.einsum('hqk,hkd->hqd', weight.astype(jnp.bfloat16), block[heads_kv:],...  68 us
    another operation x2, local copies, waits for them, and re-layouts, local(): pool_all.reshape(pool_all.shape[0], page_rows, 2 * KEY_VALUE_HEADS, HEAD_...  66.2 us
    all_to_all x1, blocking collectives, local(): lax.all_to_all(outbound, 'tok', split_axis=0, concat_axis=1, tiled=True)  59.9 us
    all_to_all x1, waiting for transfers between devices, local(): lax.all_to_all(expert_out, 'tok', split_axis=1, concat_axis=0, tiled=True)  59 us
    dot_general x12, matrix products, loop_step(): jnp.einsum('hqd,hkd->hqk', query_heads, block[:heads_kv], preferred_eleme...  52.2 us
    convert_element_type x1, local copies, waits for them, and re-layouts, local(): expert_out = jnp.einsum('erf,efd->erd', hidden, w_down, preferred_element...  52.2 us
    select_n x2, local copies, waits for them, and re-layouts, local(): jnp.take(pool_heads, page_table[member_id], axis=1)  45.8 us
  transfers between devices with their start and end apart: 4, of which 4 were waited for; matrix products, arithmetic and copies ran while one was open for 8% of the time, Pallas kernels for 0%

profile of v1, /device:TPU:0, one launch (start us, length us, event | category | flops | bytes accessed | tf_op | source)
XLA Modules:
  0.0 975.0 jit_solution(13447912749562439598)
XLA Ops:
  27.2 23.2 %all-to-all-done = bf16[4,4,64,1024]{3,1,2,0:T(4,128)(2,1)} async-done(((bf16[4,4,64,1024]{3,1,2,0:T(4,128)(2,1)}), bf16[4,4,64,1024]{3,1,2,0:T(4,128)(2,1)}, u32[]{:S(2)}, u32[]{:S(2)}) %all-to-all-start) | async-done | bytes 2097184 | tf_op jit(solution)/shard_map/all_to_all | solution.py:128
  55.3 6.1 stack.14
  61.4 8.3 all-to-all-start.1
  113.6 14.1 %all-gather.2.cloned.1.call-done = bf16[2048,2048]{1,0:T(8,128)(2,1)} async-done(((bf16[64,2048]{1,0:T(8,128)(2,1)}), bf16[2048,2048]{1,0:T(8,128)(2,1)}) %all-gather.2.cloned.1.call-update) | async-done | bytes 8388624 | tf_op jit(solution)/shard_map/all_gather | solution.py:158
  127.8 12.3 %copy.103 = bf16[2048,2048]{0,1:T(8,128)(2,1)} copy(bf16[2048,2048]{1,0:T(8,128)(2,1)} %all-gather.2.cloned.1.call-done) | data formatting | bytes 16777216 | tf_op jit(solution)/shard_map/all_gather | solution.py:158
  140.1 6.1 slice_bitcast_fusion.1
  146.2 144.3 %all-to-all-done.1 = bf16[32,4,64,1024]{3,2,1,0:T(8,128)(2,1)} async-done(((bf16[32,4,64,1024]{3,2,1,0:T(8,128)(2,1)}), bf16[32,4,64,1024]{3,2,1,0:T(8,128)(2,1)}, u32[]{:S(2)}, u32[]{:S(2)}) %all-to-all-start.1) | async-done | bytes 16777248 | tf_op jit(solution)/shard_map/all_to_all | solution.py:137
  290.4 43.1 %reshape_reshape.3 = bf16[128,64,16,64]{3,2,1,0:T(8,128)(2,1)} reshape(bf16[32,4,64,1024]{3,2,1,0:T(8,128)(2,1)} %all-to-all-done.1) | data formatting | bytes 33554432 | tf_op jit(solution)/shard_map/reshape;reshape | solution.py:139
  333.5 23.1 %copy.138 = bf16[128,64,16,64]{3,1,0,2:T(8,128)(2,1)} copy(bf16[128,64,16,64]{3,2,1,0:T(8,128)(2,1)} %reshape_reshape.3) | data formatting | bytes 33554432 | tf_op jit(solution)/shard_map/reshape;reshape | solution.py:139
  356.7 11.9 %gather_fusion.2 = bf16[64,16,64,64]{3,2,1,0:T(8,128)(2,1)} fusion(bf16[16,128,64,64]{3,2,1,0:T(8,128)(2,1)} %bitcast.229, s32[1024]{0:T(1024)S(1)} %pad_clamp_fusion.2), kind=kCustom, calls=%fused_computation.clone | custom fusion | bytes 16777472 | tf_op jit(solution)/shard_map/jit(_take)/gather | solution.py:144
  368.5 11.9 %gather_fusion.3 = bf16[64,16,64,64]{3,2,1,0:T(8,128)(2,1)} fusion(bf16[16,128,64,64]{3,2,1,0:T(8,128)(2,1)} %bitcast.230, s32[1024]{0:T(1024)S(1)} %pad_clamp_fusion.1), kind=kCustom, calls=%fused_computation.1.clone | custom fusion | bytes 16777472 | tf_op jit(solution)/shard_map/jit(_take)/gather | solution.py:144
  380.4 23.0 %select_bitcast_fusion = (bf16[16,64,64,64]{3,2,0,1:T(8,128)(2,1)}, bf16[16,64,64,64]{3,2,0,1:T(8,128)(2,1)}) fusion(bf16[64,16,64,64]{3,2,1,0:T(8,128)(2,1)} %gather_fusion.3, pred[64]{0:T(512)(128)(4,1)S(1)} %get-tuple-element.895, bf16[64,16,64,64]{3,2,1,0:T(8,128)(2,1)} %gather_fusion.2, pred[64]{0:T(512)(128)(4,1)S(1)} %get-tuple-element.873), kind=kLoop, calls=%fused_computation.92 | loop fusion | flops 8388608 | bytes 33554560 | tf_op jit(solution)/shard_map/jit(_take)/select_n | solution.py:144
  403.4 22.9 %copy.98 = bf16[16,64,64,64]{2,1,3,0:T(8,128)(2,1)} copy(bf16[16,64,64,64]{3,2,0,1:T(8,128)(2,1)} %get-tuple-element.902) | data formatting | bytes 16777216 | tf_op jit(solution)/shard_map/jit(_take)/select_n | solution.py:144
  426.3 22.6 %reshape.408 = bf16[16,4096,64]{1,2,0:T(8,128)(2,1)} reshape(bf16[16,64,64,64]{2,1,3,0:T(8,128)(2,1)} %copy.98) | data formatting | bytes 16777216 | tf_op jit(solution)/shard_map/reshape | solution.py:144
  448.9 60.4 %while.74 = (s32[]{:T(128)}, f32[8,192]{1,0:T(8,128)S(1)}, f32[8,192]{1,0:T(8,128)S(1)}, f32[8,192,64]{1,2,0:T(8,128)}, s32[4096]{0:T(1024)S(1)}, /*index=5*/bf1...) while((s32[]{:T(128)}, f32[8,192]{1,0:T(8,128)S(1)}, ...), condition=%wide.region_5.7_spmd.clone, body=%wide.region_2.6_spmd.clone.sunk | while | flops 423599616 | bytes 24100308 | solution.py:59
  509.3 27.0 %while.72 = (s32[]{:T(128)}, f32[8,192]{1,0:T(8,128)S(1)}, f32[8,192]{1,0:T(8,128)S(1)}, f32[8,192,64]{1,2,0:T(8,128)}, s32[2048]{0:T(1024)S(1)}, /*index=5*/bf1...) while((s32[]{:T(128)}, f32[8,192]{1,0:T(8,128)S(1)}, ...), condition=%wide.region_9.11_spmd.clone, body=%wide.region_6.10_spmd.clone.sunk | while | flops 423496704 | bytes 49266148 | solution.py:59
  537.0 22.9 %copy.106 = bf16[16,64,64,64]{2,1,3,0:T(8,128)(2,1)} copy(bf16[16,64,64,64]{3,2,0,1:T(8,128)(2,1)} %get-tuple-element.901) | data formatting | bytes 16777216 | tf_op jit(solution)/shard_map/jit(_take)/select_n | solution.py:144
  559.8 22.6 %reshape.412 = bf16[16,4096,64]{1,2,0:T(8,128)(2,1)} reshape(bf16[16,64,64,64]{2,1,3,0:T(8,128)(2,1)} %copy.106) | data formatting | bytes 16777216 | tf_op jit(solution)/shard_map/reshape | solution.py:144
  582.5 63.1 %while.75 = (s32[]{:T(128)}, f32[8,192]{1,0:T(8,128)S(1)}, f32[8,192]{1,0:T(8,128)S(1)}, f32[8,192,64]{1,2,0:T(8,128)}, s32[4096]{0:T(1024)}, /*index=5*/bf16[16...) while((s32[]{:T(128)}, f32[8,192]{1,0:T(8,128)S(1)}, ...), condition=%wide.region_13.15_spmd.clone, body=%wide.region_10.14_spmd.clone.sunk | while | flops 423599616 | bytes 24100308 | solution.py:59
  608.2 5.7 fusion.188
  624.0 5.7 fusion.188
  639.8 5.7 fusion.188
  645.5 27.1 %while.73 = (s32[]{:T(128)}, f32[8,192]{1,0:T(8,128)S(1)}, f32[8,192]{1,0:T(8,128)S(1)}, f32[8,192,64]{1,2,0:T(8,128)}, s32[2048]{0:T(1024)S(1)}, /*index=5*/bf1...) while((s32[]{:T(128)}, f32[8,192]{1,0:T(8,128)S(1)}, ...), condition=%wide.region_17.19_spmd.clone, body=%wide.region_14.18_spmd.clone.sunk | while | flops 423496704 | bytes 49266148 | solution.py:59
  691.5 6.2 gather_fusion
  700.5 59.9 %all_to_all.28 = bf16[32,48,1536]{2,1,0:T(8,128)(2,1)S(1)} all-to-all(bf16[32,48,1536]{2,1,0:T(8,128)(2,1)S(1)} %select_select_fusion), channel_id=1, replica_groups=mesh['req'=4,'tok'=32] {'tok'}, dimensions={0} | all-to-all | bytes 9437184 | tf_op jit(solution)/shard_map/all_to_all | solution.py:205
  768.7 52.2 %copy.141 = bf16[1,1536,1536]{2,0,1:T(2,128)(2,1)} copy(bf16[1,1536,1536]{2,1,0:T(8,128)(2,1)S(1)} %fusion.78) | data formatting | bytes 9437184 | tf_op jit(solution)/shard_map/convert_element_type | solution.py:210
  821.4 32.0 %reduce.4 = bf16[1536,1536]{1,0:T(8,128)(2,1)} reduce(bf16[1536,1,1536]{2,1,0:T(2,128)(2,1)} %bitcast.231, bf16[]{:T(256)} %broadcast.487), dimensions={1}, to_apply=%bitcast.195.reduce_sub_computation | reduce | bytes 9437186
  853.4 8.2 reshape.483
  867.5 59.0 %all-to-all-done.3 = bf16[32,2,36864]{2,1,0:T(2,128)(2,1)} async-done(((bf16[32,2,36864]{2,1,0:T(2,128)(2,1)}), bf16[32,2,36864]{2,1,0:T(2,128)(2,1)}, u32[]{:S(2)}, u32[]{:S(2)}) %all-to-all-start.3) | async-done | bytes 4718624 | tf_op jit(solution)/shard_map/all_to_all | solution.py:211
  926.5 20.2 %reshape.484 = bf16[1536,1,1536]{2,1,0:T(2,128)(2,1)} reshape(bf16[32,2,36864]{2,1,0:T(2,128)(2,1)} %all-to-all-done.3) | data formatting | bytes 9437184
  946.7 7.2 copy.139
  954.0 10.2 %gather_fusion.1 = bf16[1024,1536]{1,0:T(8,128)(2,1)} fusion(bf16[1536,1536]{1,0:T(8,128)(2,1)} %bitcast.228, s32[1024]{0:T(1024)S(1)} %broadcast_clamp_fusion), kind=kCustom, calls=%fused_computation.3 | custom fusion | bytes 6295552 | tf_op jit(solution)/shard_map/jit(_take)/gather | solution.py:212
  (265 shorter events, 268.8 us)
Async XLA Ops:
  7.2 753.2 %copy-start = (bf16[1,1536,1024]{2,1,0:T(8,128)(2,1)S(1)}, bf16[1,1536,1024]{2,1,0:T(8,128)(2,1)}, u32[]{:S(2)}) copy-start(bf16[1,1536,1024]{2,1,0:T(8,128)(2,1)} %param.36) | copy-start | bytes 9437188
  11.3 12.4 %copy-start.3 = (bf16[2,64,1536]{2,1,0:T(8,128)(2,1)S(1)}, bf16[2,64,1536]{2,1,0:T(8,128)(2,1)}, u32[]{:S(2)}) copy-start(bf16[2,64,1536]{2,1,0:T(8,128)(2,1)} %param.24) | copy-start | bytes 1179652
  11.3 12.6 %copy-start.10 = (f32[1536]{0:T(1024)S(1)}, f32[1536]{0:T(1024)}, u32[]{:S(2)}) copy-start(f32[1536]{0:T(1024)} %param.25) | copy-start | bytes 18436
  19.2 31.2 %all-to-all-start = ((bf16[4,4,64,1024]{3,1,2,0:T(4,128)(2,1)}), bf16[4,4,64,1024]{3,1,2,0:T(4,128)(2,1)}, u32[]{:S(2)}, u32[]{:S(2)}) async-start(bf16[4,4,64,1024]{3,1,2,0:T(4,128)(2,1)} %copy.94), calls=%async_computation | async-start | bytes 4194304 | tf_op jit(solution)/shard_map/all_to_all | solution.py:128
  23.8 104.0 %all-gather.2.cloned.1.call-start = ((), (), s32[]{:S(2)}) async-start(), calls=%async_computation.4 | async-start | bytes 8650752 | tf_op jit(solution)/shard_map/all_gather | solution.py:158
  61.4 229.0 %all-to-all-start.1 = ((bf16[32,4,64,1024]{3,2,1,0:T(8,128)(2,1)}), bf16[32,4,64,1024]{3,2,1,0:T(8,128)(2,1)}, u32[]{:S(2)}, u32[]{:S(2)}) async-start(bf16[32,4,64,1024]{3,2,1,0:T(8,128)(2,1)} %stack.14), calls=%async_computation.1 | async-start | bytes 33554432 | tf_op jit(solution)/shard_map/all_to_all | solution.py:137
  97.7 42.4 %copy-start.14 = (s32[2,512]{1,0:T(2,128)}, s32[2,512]{1,0:T(2,128)S(1)}, u32[]{:S(2)}) copy-start(s32[2,512]{1,0:T(2,128)S(1)} %fusion.111) | copy-start | bytes 12292
  98.5 41.6 %copy-start.11 = (s32[2,64,8]{1,2,0:T(8,128)}, s32[2,64,8]{1,2,0:T(8,128)S(1)}, u32[]{:S(2)}) copy-start(s32[2,64,8]{1,2,0:T(8,128)S(1)} %broadcast_multiply_fusion) | copy-start | bytes 12292
  98.7 0.6 copy-start.23
  99.4 40.7 %copy-start.19 = (s32[1024,1]{0,1:T(1,128)}, s32[1024,1]{0,1:T(1,128)S(1)}, u32[]{:S(2)}) copy-start(s32[1024,1]{0,1:T(1,128)S(1)} %compare_select_fusion) | copy-start | bytes 12292
  448.9 60.4 %copy-start.9 = (s32[2048]{0:T(1024)S(1)}, s32[2048]{0:T(1024)}, u32[]{:S(2)}) copy-start(s32[2048]{0:T(1024)} %iota_add_fusion.1) | copy-start | bytes 24580
  512.5 2.7 copy-start.1
  525.8 2.7 copy-start.1
  559.8 22.6 %copy-start.6 = (f32[8,192]{1,0:T(8,128)S(1)}, f32[8,192]{1,0:T(8,128)}, u32[]{:S(2)}) copy-start(f32[8,192]{1,0:T(8,128)} %custom-call.3) | copy-start | bytes 18436
  559.8 22.6 %copy-start.7 = (f32[8,192]{1,0:T(8,128)S(1)}, f32[8,192]{1,0:T(8,128)}, u32[]{:S(2)}) copy-start(f32[8,192]{1,0:T(8,128)} %custom-call.4) | copy-start | bytes 18436
  559.8 22.6 %copy-start.13 = (s32[64]{0:T(128)S(1)}, s32[64]{0:T(128)}, u32[]{:S(2)}) copy-start(s32[64]{0:T(128)} %get-tuple-element.1177) | copy-start | bytes 772
  582.5 63.1 %copy-start.8 = (s32[2048]{0:T(1024)S(1)}, s32[2048]{0:T(1024)}, u32[]{:S(2)}) copy-start(s32[2048]{0:T(1024)} %iota_add_fusion) | copy-start | bytes 24580
  648.8 2.7 copy-start.2
  662.2 2.7 copy-start.2
  672.7 14.5 %copy-start.4 = (bf16[2,64,1536]{2,1,0:T(8,128)(2,1)S(1)}, bf16[2,64,1536]{2,1,0:T(8,128)(2,1)}, u32[]{:S(2)}) copy-start(bf16[2,64,1536]{2,1,0:T(8,128)(2,1)} %param.24) | copy-start | bytes 1179652
  675.6 15.0 %copy-start.21 = (f32[1536]{0:T(1024)S(1)}, f32[1536]{0:T(1024)}, u32[]{:S(2)}) copy-start(f32[1536]{0:T(1024)} %param.33) | copy-start | bytes 18436
  678.5 12.9 %copy-start.16 = (s32[2048]{0:T(1024)S(1)}, s32[2048]{0:T(1024)}, u32[]{:S(2)}) copy-start(s32[2048]{0:T(1024)} %pad_clamp_fusion) | copy-start | bytes 24580
  687.1 3.4 copy-start.5
  691.5 6.2 copy-start.17
  691.5 6.2 copy-start.18
  760.4 5.4 copy-start.25
  861.6 5.3 copy-start.15
  861.6 5.4 copy-start.12
  861.6 5.5 copy-start.24
  861.6 5.8 copy-start.22
  861.6 5.9 copy-start.20
  861.6 64.9 %all-to-all-start.3 = ((bf16[32,2,36864]{2,1,0:T(2,128)(2,1)}), bf16[32,2,36864]{2,1,0:T(2,128)(2,1)}, u32[]{:S(2)}, u32[]{:S(2)}) async-start(bf16[32,2,36864]{2,1,0:T(2,128)(2,1)} %reshape.483), calls=%async_computation.3 | async-start | bytes 9437184 | tf_op jit(solution)/shard_map/all_to_all | solution.py:211
Sparse Core Ops, SparseCore 0:
  27.4 100.2 all-gather.1
